TPU v7x, 32 devices: a whole 2x2x4 slice. The times are simulated.
32 devices in a mesh: row: 8 (over y, x, core), col: 4 (over z).
Axes of the slice: x: 2, y: 2, z: 4, core: 2. Of those that a mesh axis runs over, the one named last changes fastest.
Arguments:
- fast_pos: float32 [3, 4096], P(None, ('row', 'col')), may hold values from 0 to 1
- fast_vel: float32 [3, 4096], P(None, ('row', 'col')), may hold values from -5 to 5
- fast_charge: float32 [4096], replicated, may hold values from -4 to 4
- fast_owner: int32 [4096], replicated, may hold values from 0 to 1023, as said below
- exclusions: int32 [4096, 4], replicated, may hold values from 0 to 4095, as said below
- slow_pos: float32 [3, 32, 32, 128], P(None, 'row', 'col'), may hold values from 0 to 1
- slow_vel: float32 [3, 32, 32, 128], P(None, 'row', 'col'), may hold values from -5 to 5
- slow_charge: float32 [32, 32, 128], P('row', 'col'), may hold values from -4 to 4
- neighbours: int32 [32, 32, 5], P('row', 'col'), may hold values from 0 to 24, all different within a row
Outputs:
- fast_pos_out: float32 [3, 4096], P(None, ('row', 'col'))
- fast_vel_out: float32 [3, 4096], P(None, ('row', 'col'))
- slow_pos_out: float32 [3, 32, 32, 128], P(None, 'row', 'col')
- slow_vel_out: float32 [3, 32, 32, 128], P(None, 'row', 'col')
Inputs may be any that keep to these rules, and one draw needn't show every extreme that they name: `fast_owner`: atoms a and b with a % (256) == b % (256) share an owner. `exclusions`: the partners of atom a are atoms b != a with b % (256) == a % 256; a partner may repeat. `neighbours`: the entries of one cell are distinct.
All inputs are finite; a program needn't handle non-finite values.
Results may differ from a plain program's by a relative error of at most 0.0003.
Values sent between devices are 32-bit elements; how exact they have to be, the bound alone decides.
No kernel may reach another device: no remote copies, remote signals or barrier semaphores. Data moves between devices by JAX's collectives and lax.ppermute only.
A program may use at most 64 MiB of HBM per device.

v0:
```python
import jax
import jax.numpy as jnp
from jax import lax
from jax.sharding import PartitionSpec as P

FAST = 4096
CELL = 128
INNER = 4
fast_coupling = 1.0
slow_coupling = 0.1
outer_dt = 0.2


def with_halo(x, sides, width):
    for axis, dim in sides:
        count, length = (lax.axis_size(axis), x.shape[dim])
        up = [(i, (i + 1) % count) for i in range(count)]
        down = [(j, i) for i, j in up]
        last = lax.slice_in_dim(x, length - width, length, axis=dim)
        initial = lax.slice_in_dim(x, 0, width, axis=dim)
        before = lax.ppermute(last, axis, up)
        after = lax.ppermute(initial, axis, down)
        x = jnp.concatenate([before, x, after], axis=dim)
    return x


def owner_coords(owner, total_cols):
    grid_row = (owner // total_cols).astype(jnp.float32)
    grid_col = (owner % total_cols).astype(jnp.float32)
    return jnp.stack([grid_row, grid_col, jnp.zeros_like(grid_row)])


def pair_fast(pos_a, cell_a, charge_a, exclude_a, pos_b, cell_b, charge_b, index_b):
    delta = pos_a[:, :, None] - pos_b[:, None, :] + (cell_a[:, :, None] - cell_b[:, None, :])
    dist_sq = jnp.sum(delta * delta, axis=0) + 1.0
    inverse = 1.0 / (dist_sq * jnp.sqrt(dist_sq))
    barred = jnp.any(exclude_a[:, :, None] == index_b[None, None, :], axis=1)
    weight = jnp.where(barred, jnp.float32(0.0), charge_a[:, None] * charge_b[None, :] * inverse)
    return fast_coupling * jnp.sum(weight[None] * delta, axis=2)


def slow_cells(own, views, lists):
    force = jnp.zeros((3,) + own.shape[1:], jnp.float32)
    offsets = jnp.arange(25, dtype=jnp.int32)
    for slot in range(lists.shape[-1]):
        chosen = lists[..., slot]
        pick = (chosen[..., None] == offsets).astype(jnp.float32)
        other = jnp.einsum("abo,oxabn->xabn", pick, views, precision=lax.Precision.HIGHEST)
        shift_row = (chosen // 5 - 2).astype(jnp.float32)
        shift_col = (chosen % 5 - 2).astype(jnp.float32)
        shift = jnp.stack([shift_row, shift_col, jnp.zeros_like(shift_row)])
        delta = own[0:3, :, :, :, None] - (other[0:3, :, :, None, :] + shift[:, :, :, None, None])
        dist_sq = jnp.sum(delta * delta, axis=0) + 0.5
        inverse = 1.0 / (dist_sq * jnp.sqrt(dist_sq))
        weight = other[3][:, :, None, :] * inverse
        force = force + jnp.sum(weight[None] * delta, axis=-1)
    return slow_coupling * own[3][None] * force


def fast_from_cells(frac, charge, picked):
    delta = frac[:, :, None] - picked[0:3]
    dist_sq = jnp.sum(delta * delta, axis=0) + 0.5
    inverse = 1.0 / (dist_sq * jnp.sqrt(dist_sq))
    weight = picked[3] * inverse
    return slow_coupling * charge[None, :] * jnp.sum(weight[None] * delta, axis=-1)


def per_device(
    fast_pos,
    fast_vel,
    fast_charge,
    fast_owner,
    exclusions,
    slow_pos,
    slow_vel,
    slow_charge,
    neighbours,
):
    row_count = lax.axis_size("row")
    col_count = lax.axis_size("col")
    row_index = lax.axis_index("row")
    col_index = lax.axis_index("col")
    flat_index = row_index * col_count + col_index
    piece = fast_pos.shape[1]
    cell_rows = slow_pos.shape[1]
    cell_cols = slow_pos.shape[2]
    total_cols = cell_cols * col_count
    coords = owner_coords(fast_owner, total_cols)
    block_width = col_count * piece
    block_start = row_index * block_width
    rows_cells = lax.dynamic_slice_in_dim(coords, block_start, block_width, 1)
    rows_charge = lax.dynamic_slice_in_dim(fast_charge, block_start, block_width, 0)
    rows_exclude = lax.dynamic_slice_in_dim(exclusions, block_start, block_width, 0)
    column_atoms = (
        (jnp.arange(row_count, dtype=jnp.int32) * col_count + col_index)[:, None] * piece
        + jnp.arange(piece, dtype=jnp.int32)[None, :]
    ).reshape(-1)
    column_cells = jnp.take(coords, column_atoms, axis=1)
    column_charge = jnp.take(fast_charge, column_atoms, axis=0)

    def fast_force(frac):
        rows_pos = lax.all_gather(frac, "col", axis=1, tiled=True)
        cols_pos = lax.all_gather(frac, "row", axis=1, tiled=True)
        partial_force = pair_fast(
            rows_pos,
            rows_cells,
            rows_charge,
            rows_exclude,
            cols_pos,
            column_cells,
            column_charge,
            column_atoms,
        )
        return lax.psum_scatter(partial_force, "col", scatter_dimension=1, tiled=True)

    grid_row = fast_owner // total_cols - row_index * cell_rows
    grid_col = fast_owner % total_cols - col_index * cell_cols
    inside = (grid_row >= 0) & (grid_row < cell_rows) & (grid_col >= 0) & (grid_col < cell_cols)
    local_cell = grid_row * cell_cols + grid_col
    cell_ids = jnp.arange(cell_rows * cell_cols, dtype=jnp.int32)
    select = jnp.where(
        inside[:, None] & (local_cell[:, None] == cell_ids[None, :]),
        jnp.float32(1.0),
        jnp.float32(0.0),
    )

    def slow_both(spos, frac):
        data = jnp.concatenate([spos, slow_charge[None]], axis=0)
        padded = with_halo(data, (("row", 1), ("col", 2)), 2)
        views = jnp.stack(
            [padded[:, o // 5 : o // 5 + cell_rows, o % 5 : o % 5 + cell_cols] for o in range(25)]
        )
        cell_force = slow_cells(data, views, neighbours)
        everyone = lax.all_gather(frac, ("row", "col"), axis=1, tiled=True)
        table = jnp.transpose(data, (1, 2, 0, 3)).reshape(cell_rows * cell_cols, 4 * CELL)
        picked = jnp.dot(
            select, table, precision=lax.Precision.HIGHEST, preferred_element_type=jnp.float32
        )
        picked = jnp.transpose(picked.reshape(FAST, 4, CELL), (1, 0, 2))
        partial_env = fast_from_cells(everyone, fast_charge, picked)
        summed = lax.psum(partial_env, ("row", "col"))
        own_env = lax.dynamic_slice_in_dim(summed, flat_index * piece, piece, 1)
        return (cell_force, own_env)

    half_outer = 0.5 * outer_dt
    inner_dt = outer_dt / INNER
    fast_acc = fast_force(fast_pos)
    slow_acc, env_acc = slow_both(slow_pos, fast_pos)
    slow_vel = slow_vel + half_outer * slow_acc
    fast_vel = fast_vel + half_outer * env_acc
    for inner_step in range(INNER):
        fast_vel = fast_vel + 0.5 * inner_dt * fast_acc
        fast_pos = fast_pos + inner_dt * fast_vel
        fast_acc = fast_force(fast_pos)
        fast_vel = fast_vel + 0.5 * inner_dt * fast_acc
    slow_pos = slow_pos + outer_dt * slow_vel
    slow_acc, env_acc = slow_both(slow_pos, fast_pos)
    slow_vel = slow_vel + half_outer * slow_acc
    fast_vel = fast_vel + half_outer * env_acc
    return (fast_pos, fast_vel, slow_pos, slow_vel)


def solution(mesh):
    return jax.shard_map(
        per_device,
        mesh=mesh,
        in_specs=(
            P(None, ("row", "col")),
            P(None, ("row", "col")),
            P(),
            P(),
            P(),
            P(None, "row", "col", None),
            P(None, "row", "col", None),
            P("row", "col", None),
            P("row", "col", None),
        ),
        out_specs=(
            P(None, ("row", "col")),
            P(None, ("row", "col")),
            P(None, "row", "col", None),
            P(None, "row", "col", None),
        ),
        check_vma=False,
    )
```

profile of v0, /device:TPU:0, one launch (start us, length us, event | category | flops | bytes accessed | tf_op | source)
XLA Modules:
  0.0 525.7 jit_solution(1581385438300912036)
XLA Ops:
  8.5 2.9 collective-permute-start.1
  11.6 9.6 %all_gather.38 = f32[3,1024]{1,0:T(4,128)S(1)} all-gather(f32[3,128]{1,0:T(4,128)} %param.9), channel_id=1, replica_groups=mesh['row'=8,'col'=4] {'row'}, dimensions={1}, use_global_device_ids=true | all-gather | bytes 13824 | tf_op jit(solution)/shard_map/all_gather | solution.py:103
  21.2 12.3 %all_gather.37 = f32[3,512]{1,0:T(4,128)S(1)} all-gather(f32[3,128]{1,0:T(4,128)} %param.9), channel_id=1, replica_groups=mesh['row'=8,'col'=4] {'col'}, dimensions={1}, use_global_device_ids=true | all-gather | bytes 7680 | tf_op jit(solution)/shard_map/all_gather | solution.py:102
  35.2 6.1 %gather_fusion = f32[1024]{0:T(1024)S(1)} fusion(f32[4096]{0:T(1024)S(1)} %copy-done.2, s32[1024]{0:T(1024)S(1)} %broadcast_clamp_fusion), kind=kCustom, calls=%fused_computation | custom fusion | bytes 12288 | tf_op jit(solution)/shard_map/jit(_take)/gather | solution.py:99
  41.3 2.8 gather_fusion.1
  51.6 65.5 %all_gather.36 = f32[3,4096]{1,0:T(4,128)S(1)} all-gather(f32[3,128]{1,0:T(4,128)S(1)} %copy-done.7), channel_id=1, replica_groups=mesh['row'=8,'col'=4] {'row','col'}, dimensions={1}, use_global_device_ids=true | all-gather | bytes 50688 | tf_op jit(solution)/shard_map/all_gather | solution.py:134
  117.2 6.8 %convolution_bitcast_fusion.1 = f32[4,4096,128]{1,2,0:T(8,128)S(1)} fusion(s32[4096]{0:T(1024)S(1)} %get-tuple-element.54, pred[4096]{0:T(1024)(128)(4,1)S(1)} %compare_and_fusion, f32[1,4,8,128]{3,2,0,1:T(8,128)S(1)} %bitcast.458, f32[3,4,8,128]{3,2,1,0:T(8,128)S(1)} %copy-done.3), kind=kOutput, calls=%fused_computation.29 | convolution fusion | flops 805715968 | bytes 8474624 | tf_op jit(solution)/shard_map/dot_general | solution.py:136
  126.9 38.7 %psum.14 = f32[3,4096]{1,0:T(4,128)S(1)} all-reduce(f32[3,4096]{1,0:T(4,128)S(1)} %broadcast_multiply_fusion.1), channel_id=1, replica_groups=mesh['row'=8,'col'=4] {'row','col'}, use_global_device_ids=true, to_apply=%region_2.3 | all-reduce | flops 12288 | bytes 98304 | tf_op jit(solution)/shard_map/psum | solution.py:141
  166.5 9.7 %all_gather.40 = f32[3,1024]{1,0:T(4,128)S(1)} all-gather(f32[3,128]{1,0:T(4,128)S(1)} %get-tuple-element.36), channel_id=1, replica_groups=mesh['row'=8,'col'=4] {'row'}, dimensions={1}, use_global_device_ids=true | all-gather | bytes 13824 | tf_op jit(solution)/shard_map/all_gather | solution.py:103
  176.2 12.1 %all_gather.39 = f32[3,512]{1,0:T(4,128)S(1)} all-gather(f32[3,128]{1,0:T(4,128)S(1)} %get-tuple-element.36), channel_id=1, replica_groups=mesh['row'=8,'col'=4] {'col'}, dimensions={1}, use_global_device_ids=true | all-gather | bytes 7680 | tf_op jit(solution)/shard_map/all_gather | solution.py:102
  193.7 17.6 %reduce-scatter.18.cloned.1.call-done = f32[128,3]{1,0:T(8,128)} async-done(((f32[512,3]{1,0:T(8,128)}), f32[128,3]{1,0:T(8,128)}) %reduce-scatter.18.cloned.1.call-update) | async-done | bytes 1552
  212.3 8.9 %all_gather.42 = f32[3,1024]{1,0:T(4,128)S(1)} all-gather(f32[3,128]{1,0:T(4,128)S(1)} %multiply_add_fusion.7), channel_id=1, replica_groups=mesh['row'=8,'col'=4] {'row'}, dimensions={1}, use_global_device_ids=true | all-gather | bytes 13824 | tf_op jit(solution)/shard_map/all_gather | solution.py:103
  221.2 11.9 %all_gather.41 = f32[3,512]{1,0:T(4,128)S(1)} all-gather(f32[3,128]{1,0:T(4,128)S(1)} %multiply_add_fusion.7), channel_id=1, replica_groups=mesh['row'=8,'col'=4] {'col'}, dimensions={1}, use_global_device_ids=true | all-gather | bytes 7680 | tf_op jit(solution)/shard_map/all_gather | solution.py:102
  238.5 3.8 collective-permute-start.3
  242.4 13.8 %reduce-scatter.20.cloned.1.call-done = f32[128,3]{1,0:T(8,128)} async-done(((f32[512,3]{1,0:T(8,128)}), f32[128,3]{1,0:T(8,128)}) %reduce-scatter.20.cloned.1.call-update) | async-done | bytes 1552
  257.1 8.9 %all_gather.44 = f32[3,1024]{1,0:T(4,128)S(1)} all-gather(f32[3,128]{1,0:T(4,128)S(1)} %get-tuple-element.34), channel_id=1, replica_groups=mesh['row'=8,'col'=4] {'row'}, dimensions={1}, use_global_device_ids=true | all-gather | bytes 13824 | tf_op jit(solution)/shard_map/all_gather | solution.py:103
  266.0 11.9 %all_gather.43 = f32[3,512]{1,0:T(4,128)S(1)} all-gather(f32[3,128]{1,0:T(4,128)S(1)} %get-tuple-element.34), channel_id=1, replica_groups=mesh['row'=8,'col'=4] {'col'}, dimensions={1}, use_global_device_ids=true | all-gather | bytes 7680 | tf_op jit(solution)/shard_map/all_gather | solution.py:102
  283.2 17.7 %reduce-scatter.22.cloned.1.call-done = f32[128,3]{1,0:T(8,128)} async-done(((f32[512,3]{1,0:T(8,128)}), f32[128,3]{1,0:T(8,128)}) %reduce-scatter.22.cloned.1.call-update) | async-done | bytes 1552
  301.8 8.9 %all_gather.46 = f32[3,1024]{1,0:T(4,128)S(1)} all-gather(f32[3,128]{1,0:T(4,128)S(1)} %multiply_add_fusion.5), channel_id=1, replica_groups=mesh['row'=8,'col'=4] {'row'}, dimensions={1}, use_global_device_ids=true | all-gather | bytes 13824 | tf_op jit(solution)/shard_map/all_gather | solution.py:103
  310.7 12.3 %all_gather.45 = f32[3,512]{1,0:T(4,128)S(1)} all-gather(f32[3,128]{1,0:T(4,128)S(1)} %multiply_add_fusion.5), channel_id=1, replica_groups=mesh['row'=8,'col'=4] {'col'}, dimensions={1}, use_global_device_ids=true | all-gather | bytes 7680 | tf_op jit(solution)/shard_map/all_gather | solution.py:102
  328.3 63.9 %all_gather.47 = f32[3,4096]{1,0:T(4,128)S(1)} all-gather(f32[3,128]{1,0:T(4,128)S(1)} %multiply_add_fusion.5), channel_id=1, replica_groups=mesh['row'=8,'col'=4] {'row','col'}, dimensions={1}, use_global_device_ids=true | all-gather | bytes 50688 | tf_op jit(solution)/shard_map/all_gather | solution.py:134
  403.4 2.5 fusion.2
  407.5 7.2 %fusion.3 = (f32[3,4,8,128]{3,2,1,0:T(8,128)S(1)}, f32[4,8,128,128]{3,2,1,0:T(8,128)S(1)}, f32[4,8,128,128]{3,2,1,0:T(8,128)S(1)}, f32[4,8,128,128]{3,2,1,0:T(8,128)S(1)}, f32[3,4,8,128]{3,2,1,0:T(8,128)S(1)}) fusion(f32[4,8,128,128]{3,2,1,0:T(8,128)S(1)} %fusion.51, f32[3,4,8,128]{3,2,1,0:T(8,128)S(1)} %slice_add_fusion.8, ...), kind=kLoop, calls=%fused_computation.33 | loop fusion | flops 21995520 | bytes 10878976 | tf_op jit(solution)/shard_map/reduce_sum | solution.py:56
  417.0 8.3 %fusion.5 = (f32[3,4,8,128]{3,2,1,0:T(8,128)S(1)}, f32[3,4,8,128]{3,2,1,0:T(8,128)S(1)}, f32[3,4,8,128]{3,2,1,0:T(8,128)S(1)}) fusion(f32[4,8,128,128]{3,2,1,0:T(8,128)S(1)} %fusion.53, f32[3,4,8,128]{3,2,1,0:T(8,128)S(1)} %slice_add_fusion.7, f32[3,4,8,128]{3,2,1,0:T(8,128)S(1)} %copy-done.3, f32[3,4,8,128]{3,2,1,0:T(8,128)S(1)} %slice_add_fusion.5, ...), kind=kLoop, calls=%fused_computation.35 | loop fusion | flops 14118912 | bytes 6635520 | tf_op jit(solution)/shard_map/reduce_sum | solution.py:56
  425.4 6.8 %convolution_bitcast_fusion = f32[4,4096,128]{1,2,0:T(8,128)S(1)} fusion(s32[4096]{0:T(1024)S(1)} %get-tuple-element.54, pred[4096]{0:T(1024)(128)(4,1)S(1)} %compare_and_fusion, f32[1,4,8,128]{3,2,1,0:T(8,128)S(1)} %bitcast.464, f32[3,4,8,128]{3,2,1,0:T(8,128)S(1)} %get-tuple-element.32), kind=kOutput, calls=%fused_computation.28 | convolution fusion | flops 805715968 | bytes 8474624 | tf_op jit(solution)/shard_map/dot_general | solution.py:136
  432.2 2.6 collective-permute-start.5
  437.6 40.2 %psum.15 = f32[3,4096]{1,0:T(4,128)S(1)} all-reduce(f32[3,4096]{1,0:T(4,128)S(1)} %broadcast_multiply_fusion), channel_id=1, replica_groups=mesh['row'=8,'col'=4] {'row','col'}, use_global_device_ids=true, to_apply=%region_31.32 | all-reduce | flops 12288 | bytes 98304 | tf_op jit(solution)/shard_map/psum | solution.py:141
  478.4 4.2 collective-permute-start.7
  484.7 2.3 fusion.28
  496.6 2.5 fusion.12
  500.7 7.2 %fusion.13 = (f32[3,4,8,128]{3,2,1,0:T(8,128)S(1)}, f32[4,8,128,128]{3,2,1,0:T(8,128)S(1)}, f32[4,8,128,128]{3,2,1,0:T(8,128)S(1)}, f32[4,8,128,128]{3,2,1,0:T(8,128)S(1)}, f32[3,4,8,128]{3,2,1,0:T(8,128)S(1)}) fusion(f32[4,8,128,128]{3,2,1,0:T(8,128)S(1)} %fusion.64, f32[3,4,8,128]{3,2,1,0:T(8,128)S(1)} %slice_add_fusion.3, ...), kind=kLoop, calls=%fused_computation.43 | loop fusion | flops 21995520 | bytes 10878976 | tf_op jit(solution)/shard_map/reduce_sum | solution.py:56
  510.2 8.1 %fusion.15 = (f32[3,4,8,128]{3,2,1,0:T(8,128)S(1)}, f32[3,4,8,128]{3,2,1,0:T(8,128)S(1)}, f32[3,4,8,128]{3,2,1,0:T(8,128)S(1)}) fusion(f32[4,8,128,128]{3,2,1,0:T(8,128)S(1)} %fusion.66, f32[3,4,8,128]{3,2,1,0:T(8,128)S(1)} %slice_add_fusion.2, f32[3,4,8,128]{3,2,1,0:T(8,128)S(1)} %get-tuple-element.32, f32[3,4,8,128]{3,2,1,0:T(8,128)S(1)} %slice_add_fusion, ...), kind=kLoop, calls=%fused_computation.45 | loop fusion | flops 14118912 | bytes 6635520 | tf_op jit(solution)/shard_map/reduce_sum | solution.py:56
  (220 shorter events, 72.3 us)
Async XLA Ops:
  7.2 37.4 %copy-start = (s32[4096,4]{0,1:T(4,128)S(1)}, s32[4096,4]{0,1:T(4,128)}, u32[]{:S(2)}) copy-start(s32[4096,4]{0,1:T(4,128)} %param.13) | copy-start | bytes 196612
  7.2 27.9 %copy-start.2 = (f32[4096]{0:T(1024)S(1)}, f32[4096]{0:T(1024)}, u32[]{:S(2)}) copy-start(f32[4096]{0:T(1024)} %param.11) | copy-start | bytes 49156
  7.2 158.4 %reduce-scatter.16.cloned.1.call-start = ((), (), s32[]{:S(2)}) async-start(), calls=%async_computation.5 | async-start | bytes 327680
  8.0 230.4 %collective-permute-start = (f32[4,2,8,128]{3,2,0,1:T(8,128)S(1)}, f32[4,2,8,128]{3,2,0,1:T(8,128)S(1)}, u32[]{:S(2)}, u32[]{:S(2)}) collective-permute-start(f32[4,2,8,128]{3,2,0,1:T(8,128)S(1)} %get-tuple-element.52), channel_id=1, source_target_pairs={{0,4},{4,8},{8,12},{12,16},{16,20},{20,24},{24,28},{28,0},{1,5},{5... | collective-permute-start | bytes 98312 | tf_op jit(solution)/shard_map/ppermute | solution.py:21
  8.5 229.9 %collective-permute-start.1 = (f32[4,2,8,128]{3,2,0,1:T(8,128)S(1)}, f32[4,2,8,128]{3,2,0,1:T(8,128)S(1)}, u32[]{:S(2)}, u32[]{:S(2)}) collective-permute-start(f32[4,2,8,128]{3,2,0,1:T(8,128)S(1)} %get-tuple-element.53), channel_id=1, source_target_pairs={{4,0},{8,4},{12,8},{16,12},{20,16},{24,20},{28,24},{0,28},{5,1},{9... | collective-permute-start | bytes 98312 | tf_op jit(solution)/shard_map/ppermute | solution.py:22
  49.0 2.5 copy-start.9
  49.0 2.5 copy-start.5
  49.0 2.6 copy-start.6
  49.0 2.6 copy-start.7
  49.0 68.1 %copy-start.3 = (f32[3,4,8,128]{3,2,1,0:T(8,128)S(1)}, f32[3,4,8,128]{3,2,1,0:T(8,128)}, u32[]{:S(2)}) copy-start(f32[3,4,8,128]{3,2,1,0:T(8,128)} %param.14) | copy-start | bytes 147460
  51.4 160.0 %reduce-scatter.18.cloned.1.call-start = ((), (), s32[]{:S(2)}) async-start(), calls=%async_computation.6 | async-start | bytes 327680
  125.6 40.9 %copy-start.11 = (f32[3,128]{1,0:T(4,128)S(1)}, f32[3,128]{1,0:T(4,128)}, u32[]{:S(2)}) copy-start(f32[3,128]{1,0:T(4,128)} %param.10) | copy-start | bytes 4612
  193.6 62.5 %reduce-scatter.20.cloned.1.call-start = ((), (), s32[]{:S(2)}) async-start(), calls=%async_computation.7 | async-start | bytes 327680
  238.4 62.5 %reduce-scatter.22.cloned.1.call-start = ((), (), s32[]{:S(2)}) async-start(), calls=%async_computation.8 | async-start | bytes 327680
  238.5 154.7 %collective-permute-start.2 = (f32[4,8,2,128]{3,2,0,1:T(2,128)S(1)}, f32[4,8,2,128]{3,2,0,1:T(2,128)S(1)}, u32[]{:S(2)}, u32[]{:S(2)}) collective-permute-start(f32[4,8,2,128]{3,2,0,1:T(2,128)S(1)} %get-tuple-element.45), channel_id=1, source_target_pairs={{0,1},{1,2},{2,3},{3,0},{4,5},{5,6},{6,7},{7,4},{8,9},{9,10},{10,1... | collective-permute-start | bytes 98312 | tf_op jit(solution)/shard_map/ppermute | solution.py:21
  238.5 154.6 %collective-permute-start.3 = (f32[4,8,2,128]{3,2,0,1:T(2,128)S(1)}, f32[4,8,2,128]{3,2,0,1:T(2,128)S(1)}, u32[]{:S(2)}, u32[]{:S(2)}) collective-permute-start(f32[4,8,2,128]{3,2,0,1:T(2,128)S(1)} %get-tuple-element.44), channel_id=1, source_target_pairs={{1,0},{2,1},{3,2},{0,3},{5,4},{6,5},{7,6},{4,7},{9,8},{10,9},{11,1... | collective-permute-start | bytes 98312 | tf_op jit(solution)/shard_map/ppermute | solution.py:22
  283.2 109.1 %reduce-scatter.24.cloned.1.call-start = ((), (), s32[]{:S(2)}) async-start(), calls=%async_computation.9 | async-start | bytes 327680
  301.8 26.5 %copy-start.10 = (f32[3,128]{1,0:T(4,128)}, f32[3,128]{1,0:T(4,128)S(1)}, u32[]{:S(2)}) copy-start(f32[3,128]{1,0:T(4,128)S(1)} %multiply_add_fusion.5) | copy-start | bytes 4612
  417.0 8.3 %copy-start.8 = (f32[3,4,8,128]{3,2,1,0:T(8,128)S(1)}, f32[3,4,8,128]{3,2,1,0:T(8,128)}, u32[]{:S(2)}) copy-start(f32[3,4,8,128]{3,2,1,0:T(8,128)} %param.15) | copy-start | bytes 147460
  425.3 84.9 %copy-start.4 = (f32[3,4,8,128]{3,2,1,0:T(8,128)}, f32[3,4,8,128]{3,2,1,0:T(8,128)S(1)}, u32[]{:S(2)}) copy-start(f32[3,4,8,128]{3,2,1,0:T(8,128)S(1)} %get-tuple-element.32) | copy-start | bytes 147460
  432.2 46.2 %collective-permute-start.4 = (f32[4,2,8,128]{3,2,1,0:T(8,128)S(1)}, f32[4,2,8,128]{3,2,1,0:T(8,128)S(1)}, u32[]{:S(2)}, u32[]{:S(2)}) collective-permute-start(f32[4,2,8,128]{3,2,1,0:T(8,128)S(1)} %get-tuple-element.48), channel_id=1, source_target_pairs={{0,4},{4,8},{8,12},{12,16},{16,20},{20,24},{24,28},{28,0},{1,5},{5... | collective-permute-start | bytes 98312 | tf_op jit(solution)/shard_map/ppermute | solution.py:21
  432.2 46.1 %collective-permute-start.5 = (f32[4,2,8,128]{3,2,1,0:T(8,128)S(1)}, f32[4,2,8,128]{3,2,1,0:T(8,128)S(1)}, u32[]{:S(2)}, u32[]{:S(2)}) collective-permute-start(f32[4,2,8,128]{3,2,1,0:T(8,128)S(1)} %get-tuple-element.49), channel_id=1, source_target_pairs={{4,0},{8,4},{12,8},{16,12},{20,16},{24,20},{28,24},{0,28},{5,1},{9... | collective-permute-start | bytes 98312 | tf_op jit(solution)/shard_map/ppermute | solution.py:22
  478.4 5.8 %collective-permute-start.6 = (f32[4,8,2,128]{3,2,1,0:T(2,128)S(1)}, f32[4,8,2,128]{3,2,1,0:T(2,128)S(1)}, u32[]{:S(2)}, u32[]{:S(2)}) collective-permute-start(f32[4,8,2,128]{3,2,1,0:T(2,128)S(1)} %get-tuple-element.41), channel_id=1, source_target_pairs={{0,1},{1,2},{2,3},{3,0},{4,5},{5,6},{6,7},{7,4},{8,9},{9,10},{10,1... | collective-permute-start | bytes 98312 | tf_op jit(solution)/shard_map/ppermute | solution.py:21
  478.4 5.8 %collective-permute-start.7 = (f32[4,8,2,128]{3,2,1,0:T(2,128)S(1)}, f32[4,8,2,128]{3,2,1,0:T(2,128)S(1)}, u32[]{:S(2)}, u32[]{:S(2)}) collective-permute-start(f32[4,8,2,128]{3,2,1,0:T(2,128)S(1)} %get-tuple-element.40), channel_id=1, source_target_pairs={{1,0},{2,1},{3,2},{0,3},{5,4},{6,5},{7,6},{4,7},{9,8},{10,9},{11,1... | collective-permute-start | bytes 98312 | tf_op jit(solution)/shard_map/ppermute | solution.py:22
  509.4 9.5 %copy-start.1 = (s32[4096,4]{0,1:T(4,128)S(1)}, s32[4096,4]{0,1:T(4,128)}, u32[]{:S(2)}) copy-start(s32[4096,4]{0,1:T(4,128)} %param.13) | copy-start | bytes 196612
Sparse Core Ops, SparseCore 0:
  51.5 18.8 reduce-scatter.15
  193.7 17.5 reduce-scatter.17
  238.5 17.6 reduce-scatter.19
  283.3 17.5 reduce-scatter.21
  328.4 17.6 reduce-scatter.23
where the time goes:
time: 531 us; the launch traced here: 526 us
  blocking collectives  315 us (59%)
  other arithmetic  76.8 us (14%)
  waiting for transfers between devices  50.8 us (10%)
  matrix products  34.2 us (6%)
  local copies, waits for them, and re-layouts  19.3 us (4%)
  between operations  15.2 us (3%)
  starting transfers between devices  14.4 us (3%)
    all_gather x2, blocking collectives, slow_both(): everyone = lax.all_gather(frac, ('row', 'col'), axis=1, tiled=True)  129 us
    psum x2, blocking collectives, slow_both(): summed = lax.psum(partial_env, ('row', 'col'))  78.8 us
    all_gather x5, blocking collectives, fast_force(): rows_pos = lax.all_gather(frac, 'col', axis=1, tiled=True)  60.6 us
    unnamed x10, waiting for transfers between devices  49.2 us
    all_gather x5, blocking collectives, fast_force(): cols_pos = lax.all_gather(frac, 'row', axis=1, tiled=True)  45.9 us
    reduce_sum x4, other arithmetic, slow_cells(): force = force + jnp.sum(weight[None] * delta, axis=-1)  30.7 us
    dot_general x10, matrix products, slow_cells(): jnp.einsum('abo,oxabn->xabn', pick, views, precision=lax.Precision.HIGHEST)  20.6 us
    dot_general x2, matrix products, slow_both(): jnp.dot(select, table, precision=lax.Precision.HIGHEST, preferred_element...  13.6 us
  transfers between devices with their start and end apart: 13, of which 5 were waited for; matrix products, arithmetic and copies ran while one was open for 11% of the time, Pallas kernels for 0%

commit v1 on v0

--- a/solution.py
+++ b/solution.py
@@ -138,7 +138,7 @@
         )
         picked = jnp.transpose(picked.reshape(FAST, 4, CELL), (1, 0, 2))
         partial_env = fast_from_cells(everyone, fast_charge, picked)
-        summed = lax.psum(partial_env, ("row", "col"))
+        summed = lax.all_gather(partial_env, axis_name=("row", "col")).sum(axis=0)
         own_env = lax.dynamic_slice_in_dim(summed, flat_index * piece, piece, 1)
         return (cell_force, own_env)
 

time: 531 us -> 513 us (0.966)
  blocking collectives: 315 us -> 234 us
  waiting for transfers between devices: 50.8 us -> 92.7 us
  other arithmetic: 76.8 us -> 92.3 us
    psum x2 -> x0, blocking collectives: 78.8 us -> none  [slow_both(): summed = lax.psum(partial_env, ('row', 'col'))]
    all_gather x0 -> x2, waiting for transfers between devices: none -> 34.8 us  [slow_both(): summed = lax.all_gather(partial_env, axis_name=('row', 'col')).sum(axis=0)]
    unnamed x10 -> x12, waiting for transfers between devices: 49.2 us -> 54.6 us
  transfers between devices with their start and end apart: 13 -> 15, of which waited for: 5 -> 7; matrix products, arithmetic and copies ran while one was open for 11% -> 23% of each run, Pallas kernels for 0% -> 0%
where the time goes in v1:
time: 513 us; the launch traced here: 507 us
  blocking collectives  234 us (46%)
  waiting for transfers between devices  92.7 us (18%)
  other arithmetic  92.3 us (18%)
  matrix products  36.4 us (7%)
  local copies, waits for them, and re-layouts  19.5 us (4%)
  between operations  16.7 us (3%)
  starting transfers between devices  15.1 us (3%)
    all_gather x2, blocking collectives, slow_both(): everyone = lax.all_gather(frac, ('row', 'col'), axis=1, tiled=True)  130 us
    all_gather x5, blocking collectives, fast_force(): rows_pos = lax.all_gather(frac, 'col', axis=1, tiled=True)  60.4 us
    unnamed x12, waiting for transfers between devices  54.6 us
    all_gather x5, blocking collectives, fast_force(): cols_pos = lax.all_gather(frac, 'row', axis=1, tiled=True)  44.3 us
    all_gather x2, waiting for transfers between devices, slow_both(): summed = lax.all_gather(partial_env, axis_name=('row', 'col')).sum(axis=0)  34.8 us
    reduce_sum x4, other arithmetic, slow_cells(): force = force + jnp.sum(weight[None] * delta, axis=-1)  32.1 us
    dot_general x10, matrix products, slow_cells(): jnp.einsum('abo,oxabn->xabn', pick, views, precision=lax.Precision.HIGHEST)  20.6 us
    dot_general x2, matrix products, slow_both(): jnp.dot(select, table, precision=lax.Precision.HIGHEST, preferred_element...  15.8 us
  transfers between devices with their start and end apart: 15, of which 7 were waited for; matrix products, arithmetic and copies ran while one was open for 23% of the time, Pallas kernels for 0%

profile of v1, /device:TPU:0, one launch (start us, length us, event | category | flops | bytes accessed | tf_op | source)
XLA Modules:
  0.0 507.0 jit_solution(17144930354687698313)
XLA Ops:
  9.4 2.9 collective-permute-start.1
  12.4 9.6 %all_gather.47 = f32[3,1024]{1,0:T(4,128)S(1)} all-gather(f32[3,128]{1,0:T(4,128)} %param.9), channel_id=1, replica_groups=mesh['row'=8,'col'=4] {'row'}, dimensions={1}, use_global_device_ids=true | all-gather | bytes 13824 | tf_op jit(solution)/shard_map/all_gather | solution.py:103
  22.1 12.3 %all_gather.46 = f32[3,512]{1,0:T(4,128)S(1)} all-gather(f32[3,128]{1,0:T(4,128)} %param.9), channel_id=1, replica_groups=mesh['row'=8,'col'=4] {'col'}, dimensions={1}, use_global_device_ids=true | all-gather | bytes 7680 | tf_op jit(solution)/shard_map/all_gather | solution.py:102
  36.0 6.1 %gather_fusion = f32[1024]{0:T(1024)S(1)} fusion(f32[4096]{0:T(1024)S(1)} %copy-done.2, s32[1024]{0:T(1024)S(1)} %broadcast_clamp_fusion), kind=kCustom, calls=%fused_computation | custom fusion | bytes 12288 | tf_op jit(solution)/shard_map/jit(_take)/gather | solution.py:99
  42.2 2.8 gather_fusion.1
  52.4 65.9 %all_gather.44 = f32[3,4096]{1,0:T(4,128)S(1)} all-gather(f32[3,128]{1,0:T(4,128)S(1)} %copy-done.7), channel_id=1, replica_groups=mesh['row'=8,'col'=4] {'row','col'}, dimensions={1}, use_global_device_ids=true | all-gather | bytes 50688 | tf_op jit(solution)/shard_map/all_gather | solution.py:134
  118.3 6.8 %convolution_bitcast_fusion.1 = f32[4,4096,128]{1,2,0:T(8,128)S(1)} fusion(s32[4096]{0:T(1024)S(1)} %get-tuple-element.54, pred[4096]{0:T(1024)(128)(4,1)S(1)} %compare_and_fusion, f32[1,4,8,128]{3,2,0,1:T(8,128)S(1)} %bitcast.462, f32[3,4,8,128]{3,2,1,0:T(8,128)S(1)} %copy-done.3), kind=kOutput, calls=%fused_computation.29 | convolution fusion | flops 805715968 | bytes 8474624 | tf_op jit(solution)/shard_map/dot_general | solution.py:136
  130.6 3.3 collective-permute-start.3
  145.8 2.5 fusion.2
  149.9 7.2 %fusion.3 = (f32[3,4,8,128]{3,2,1,0:T(8,128)S(1)}, f32[4,8,128,128]{3,2,1,0:T(8,128)S(1)}, f32[4,8,128,128]{3,2,1,0:T(8,128)S(1)}, f32[4,8,128,128]{3,2,1,0:T(8,128)S(1)}, f32[3,4,8,128]{3,2,1,0:T(8,128)S(1)}) fusion(f32[4,8,128,128]{3,2,1,0:T(8,128)S(1)} %fusion.51, f32[3,4,8,128]{3,2,1,0:T(8,128)S(1)} %slice_add_fusion.8, ...), kind=kLoop, calls=%fused_computation.33 | loop fusion | flops 21995520 | bytes 10878976 | tf_op jit(solution)/shard_map/reduce_sum | solution.py:56
  159.4 8.1 %fusion.5 = (f32[3,4,8,128]{3,2,1,0:T(8,128)S(1)}, f32[3,4,8,128]{3,2,1,0:T(8,128)S(1)}, f32[3,4,8,128]{3,2,1,0:T(8,128)S(1)}) fusion(f32[4,8,128,128]{3,2,1,0:T(8,128)S(1)} %fusion.53, f32[3,4,8,128]{3,2,1,0:T(8,128)S(1)} %slice_add_fusion.7, f32[3,4,8,128]{3,2,1,0:T(8,128)S(1)} %copy-done.3, f32[3,4,8,128]{3,2,1,0:T(8,128)S(1)} %slice_add_fusion.5, ...), kind=kLoop, calls=%fused_computation.35 | loop fusion | flops 14118912 | bytes 6635520 | tf_op jit(solution)/shard_map/reduce_sum | solution.py:56
  167.6 2.6 collective-permute-start.5
  170.2 9.0 %convolution_bitcast_fusion = f32[4,4096,128]{1,2,0:T(8,128)} fusion(s32[4096]{0:T(1024)S(1)} %get-tuple-element.54, pred[4096]{0:T(1024)(128)(4,1)S(1)} %compare_and_fusion, f32[1,4,8,128]{3,2,1,0:T(8,128)S(1)} %bitcast.468, f32[3,4,8,128]{3,2,1,0:T(8,128)S(1)} %get-tuple-element.32), kind=kOutput, calls=%fused_computation.28 | convolution fusion | flops 805715968 | bytes 8474624 | tf_op jit(solution)/shard_map/dot_general | solution.py:136
  179.3 4.6 collective-permute-start.7
  197.8 2.5 fusion.12
  205.2 8.0 %all_gather.49 = f32[3,1024]{1,0:T(4,128)S(1)} all-gather(f32[3,128]{1,0:T(4,128)S(1)} %get-tuple-element.36), channel_id=1, replica_groups=mesh['row'=8,'col'=4] {'row'}, dimensions={1}, use_global_device_ids=true | all-gather | bytes 13824 | tf_op jit(solution)/shard_map/all_gather | solution.py:103
  213.2 12.4 %all_gather.48 = f32[3,512]{1,0:T(4,128)S(1)} all-gather(f32[3,128]{1,0:T(4,128)S(1)} %get-tuple-element.36), channel_id=1, replica_groups=mesh['row'=8,'col'=4] {'col'}, dimensions={1}, use_global_device_ids=true | all-gather | bytes 7680 | tf_op jit(solution)/shard_map/all_gather | solution.py:102
  231.0 19.1 %reduce-scatter.18.cloned.1.call-done = f32[128,3]{1,0:T(8,128)} async-done(((f32[512,3]{1,0:T(8,128)}), f32[128,3]{1,0:T(8,128)}) %reduce-scatter.18.cloned.1.call-update) | async-done | bytes 1552
  251.0 8.9 %all_gather.51 = f32[3,1024]{1,0:T(4,128)S(1)} all-gather(f32[3,128]{1,0:T(4,128)S(1)} %multiply_add_fusion.7), channel_id=1, replica_groups=mesh['row'=8,'col'=4] {'row'}, dimensions={1}, use_global_device_ids=true | all-gather | bytes 13824 | tf_op jit(solution)/shard_map/all_gather | solution.py:103
  259.9 11.9 %all_gather.50 = f32[3,512]{1,0:T(4,128)S(1)} all-gather(f32[3,128]{1,0:T(4,128)S(1)} %multiply_add_fusion.7), channel_id=1, replica_groups=mesh['row'=8,'col'=4] {'col'}, dimensions={1}, use_global_device_ids=true | all-gather | bytes 7680 | tf_op jit(solution)/shard_map/all_gather | solution.py:102
  277.2 17.7 %reduce-scatter.20.cloned.1.call-done = f32[128,3]{1,0:T(8,128)} async-done(((f32[512,3]{1,0:T(8,128)}), f32[128,3]{1,0:T(8,128)}) %reduce-scatter.20.cloned.1.call-update) | async-done | bytes 1552
  295.8 8.9 %all_gather.53 = f32[3,1024]{1,0:T(4,128)S(1)} all-gather(f32[3,128]{1,0:T(4,128)S(1)} %get-tuple-element.34), channel_id=1, replica_groups=mesh['row'=8,'col'=4] {'row'}, dimensions={1}, use_global_device_ids=true | all-gather | bytes 13824 | tf_op jit(solution)/shard_map/all_gather | solution.py:103
  304.7 11.9 %all_gather.52 = f32[3,512]{1,0:T(4,128)S(1)} all-gather(f32[3,128]{1,0:T(4,128)S(1)} %get-tuple-element.34), channel_id=1, replica_groups=mesh['row'=8,'col'=4] {'col'}, dimensions={1}, use_global_device_ids=true | all-gather | bytes 7680 | tf_op jit(solution)/shard_map/all_gather | solution.py:102
  322.2 17.7 %reduce-scatter.22.cloned.1.call-done = f32[128,3]{1,0:T(8,128)} async-done(((f32[512,3]{1,0:T(8,128)}), f32[128,3]{1,0:T(8,128)}) %reduce-scatter.22.cloned.1.call-update) | async-done | bytes 1552
  340.9 8.9 %all_gather.55 = f32[3,1024]{1,0:T(4,128)S(1)} all-gather(f32[3,128]{1,0:T(4,128)S(1)} %multiply_add_fusion.5), channel_id=1, replica_groups=mesh['row'=8,'col'=4] {'row'}, dimensions={1}, use_global_device_ids=true | all-gather | bytes 13824 | tf_op jit(solution)/shard_map/all_gather | solution.py:103
  349.7 11.9 %all_gather.54 = f32[3,512]{1,0:T(4,128)S(1)} all-gather(f32[3,128]{1,0:T(4,128)S(1)} %multiply_add_fusion.5), channel_id=1, replica_groups=mesh['row'=8,'col'=4] {'col'}, dimensions={1}, use_global_device_ids=true | all-gather | bytes 7680 | tf_op jit(solution)/shard_map/all_gather | solution.py:102
  361.7 63.8 %all_gather.56 = f32[3,4096]{1,0:T(4,128)S(1)} all-gather(f32[3,128]{1,0:T(4,128)S(1)} %multiply_add_fusion.5), channel_id=1, replica_groups=mesh['row'=8,'col'=4] {'row','col'}, dimensions={1}, use_global_device_ids=true | all-gather | bytes 50688 | tf_op jit(solution)/shard_map/all_gather | solution.py:134
  430.8 3.9 multiply_reduce_fusion.1
  437.1 3.9 multiply_reduce_fusion
  441.7 8.7 %fusion.13 = (f32[3,4,8,128]{3,2,1,0:T(8,128)S(1)}, f32[4,8,128,128]{3,2,1,0:T(8,128)S(1)}, f32[4,8,128,128]{3,2,1,0:T(8,128)S(1)}, f32[4,8,128,128]{3,2,1,0:T(8,128)S(1)}, f32[3,4,8,128]{3,2,1,0:T(8,128)S(1)}) fusion(f32[4,8,128,128]{3,2,1,0:T(8,128)} %fusion.64, f32[3,4,8,128]{3,2,1,0:T(8,128)S(1)} %slice_add_fusion.3, ...), kind=kLoop, calls=%fused_computation.43 | loop fusion | flops 21995520 | bytes 10878976 | tf_op jit(solution)/shard_map/reduce_sum | solution.py:56
  452.7 8.1 %fusion.15 = (f32[3,4,8,128]{3,2,1,0:T(8,128)S(1)}, f32[3,4,8,128]{3,2,1,0:T(8,128)S(1)}, f32[3,4,8,128]{3,2,1,0:T(8,128)S(1)}) fusion(f32[4,8,128,128]{3,2,1,0:T(8,128)S(1)} %fusion.66, f32[3,4,8,128]{3,2,1,0:T(8,128)S(1)} %slice_add_fusion.2, f32[3,4,8,128]{3,2,1,0:T(8,128)S(1)} %get-tuple-element.32, f32[3,4,8,128]{3,2,1,0:T(8,128)S(1)} %slice_add_fusion, ...), kind=kLoop, calls=%fused_computation.45 | loop fusion | flops 14118912 | bytes 6635520 | tf_op jit(solution)/shard_map/reduce_sum | solution.py:56
  462.4 34.8 %all-gather.5.cloned.1.call-done = f32[32,3,4096]{2,1,0:T(4,128)} async-done(((f32[1,3,4096]{2,1,0:T(4,128)}), f32[32,3,4096]{2,1,0:T(4,128)}) %all-gather.5.cloned.1.call-update) | async-done | bytes 1572880 | tf_op jit(solution)/shard_map/all_gather | solution.py:141
  (226 shorter events, 83.6 us)
Async XLA Ops:
  8.0 37.4 %copy-start = (s32[4096,4]{0,1:T(4,128)S(1)}, s32[4096,4]{0,1:T(4,128)}, u32[]{:S(2)}) copy-start(s32[4096,4]{0,1:T(4,128)} %param.13) | copy-start | bytes 196612
  8.0 27.9 %copy-start.2 = (f32[4096]{0:T(1024)S(1)}, f32[4096]{0:T(1024)}, u32[]{:S(2)}) copy-start(f32[4096]{0:T(1024)} %param.11) | copy-start | bytes 49156
  8.0 120.8 %reduce-scatter.16.cloned.1.call-start = ((), (), s32[]{:S(2)}) async-start(), calls=%async_computation.7 | async-start | bytes 327680
  8.9 120.9 %collective-permute-start = (f32[4,2,8,128]{3,2,0,1:T(8,128)S(1)}, f32[4,2,8,128]{3,2,0,1:T(8,128)S(1)}, u32[]{:S(2)}, u32[]{:S(2)}) collective-permute-start(f32[4,2,8,128]{3,2,0,1:T(8,128)S(1)} %get-tuple-element.52), channel_id=1, source_target_pairs={{0,4},{4,8},{8,12},{12,16},{16,20},{20,24},{24,28},{28,0},{1,5},{5... | collective-permute-start | bytes 98312 | tf_op jit(solution)/shard_map/ppermute | solution.py:21
  9.4 120.4 %collective-permute-start.1 = (f32[4,2,8,128]{3,2,0,1:T(8,128)S(1)}, f32[4,2,8,128]{3,2,0,1:T(8,128)S(1)}, u32[]{:S(2)}, u32[]{:S(2)}) collective-permute-start(f32[4,2,8,128]{3,2,0,1:T(8,128)S(1)} %get-tuple-element.53), channel_id=1, source_target_pairs={{4,0},{8,4},{12,8},{16,12},{20,16},{24,20},{28,24},{0,28},{5,1},{9... | collective-permute-start | bytes 98312 | tf_op jit(solution)/shard_map/ppermute | solution.py:22
  49.8 2.5 copy-start.6
  49.8 2.5 copy-start.7
  49.8 68.4 %copy-start.3 = (f32[3,4,8,128]{3,2,1,0:T(8,128)S(1)}, f32[3,4,8,128]{3,2,1,0:T(8,128)}, u32[]{:S(2)}) copy-start(f32[3,4,8,128]{3,2,1,0:T(8,128)} %param.14) | copy-start | bytes 147460
  49.8 68.4 %copy-start.5 = (f32[4,8,128]{2,1,0:T(8,128)S(1)}, f32[4,8,128]{2,1,0:T(8,128)}, u32[]{:S(2)}) copy-start(f32[4,8,128]{2,1,0:T(8,128)} %param.16) | copy-start | bytes 49156
  52.2 151.0 %all-gather.3.cloned.1.call-start = ((), (), s32[]{:S(2)}) async-start(), calls=%async_computation.5 | async-start | bytes 2162688 | tf_op jit(solution)/shard_map/all_gather | solution.py:141
  126.7 1.8 copy-start.9
  128.4 121.7 %reduce-scatter.18.cloned.1.call-start = ((), (), s32[]{:S(2)}) async-start(), calls=%async_computation.8 | async-start | bytes 327680
  129.8 5.8 %collective-permute-start.2 = (f32[4,8,2,128]{3,2,0,1:T(2,128)S(1)}, f32[4,8,2,128]{3,2,0,1:T(2,128)S(1)}, u32[]{:S(2)}, u32[]{:S(2)}) collective-permute-start(f32[4,8,2,128]{3,2,0,1:T(2,128)S(1)} %get-tuple-element.45), channel_id=1, source_target_pairs={{0,1},{1,2},{2,3},{3,0},{4,5},{5,6},{6,7},{7,4},{8,9},{9,10},{10,1... | collective-permute-start | bytes 98312 | tf_op jit(solution)/shard_map/ppermute | solution.py:21
  130.6 5.0 collective-permute-start.3
  159.4 8.1 %copy-start.8 = (f32[3,4,8,128]{3,2,1,0:T(8,128)S(1)}, f32[3,4,8,128]{3,2,1,0:T(8,128)}, u32[]{:S(2)}) copy-start(f32[3,4,8,128]{3,2,1,0:T(8,128)} %param.15) | copy-start | bytes 147460
  167.5 285.2 %copy-start.4 = (f32[3,4,8,128]{3,2,1,0:T(8,128)}, f32[3,4,8,128]{3,2,1,0:T(8,128)S(1)}, u32[]{:S(2)}) copy-start(f32[3,4,8,128]{3,2,1,0:T(8,128)S(1)} %get-tuple-element.32) | copy-start | bytes 147460
  167.5 11.7 %collective-permute-start.4 = (f32[4,2,8,128]{3,2,1,0:T(8,128)S(1)}, f32[4,2,8,128]{3,2,1,0:T(8,128)S(1)}, u32[]{:S(2)}, u32[]{:S(2)}) collective-permute-start(f32[4,2,8,128]{3,2,1,0:T(8,128)S(1)} %get-tuple-element.48), channel_id=1, source_target_pairs={{0,4},{4,8},{8,12},{12,16},{16,20},{20,24},{24,28},{28,0},{1,5},{5... | collective-permute-start | bytes 98312 | tf_op jit(solution)/shard_map/ppermute | solution.py:21
  167.6 11.6 %collective-permute-start.5 = (f32[4,2,8,128]{3,2,1,0:T(8,128)S(1)}, f32[4,2,8,128]{3,2,1,0:T(8,128)S(1)}, u32[]{:S(2)}, u32[]{:S(2)}) collective-permute-start(f32[4,2,8,128]{3,2,1,0:T(8,128)S(1)} %get-tuple-element.49), channel_id=1, source_target_pairs={{4,0},{8,4},{12,8},{16,12},{20,16},{24,20},{28,24},{0,28},{5,1},{9... | collective-permute-start | bytes 98312 | tf_op jit(solution)/shard_map/ppermute | solution.py:22
  179.2 6.1 %collective-permute-start.6 = (f32[4,8,2,128]{3,2,1,0:T(2,128)S(1)}, f32[4,8,2,128]{3,2,1,0:T(2,128)S(1)}, u32[]{:S(2)}, u32[]{:S(2)}) collective-permute-start(f32[4,8,2,128]{3,2,1,0:T(2,128)S(1)} %get-tuple-element.41), channel_id=1, source_target_pairs={{0,1},{1,2},{2,3},{3,0},{4,5},{5,6},{6,7},{7,4},{8,9},{9,10},{10,1... | collective-permute-start | bytes 98312 | tf_op jit(solution)/shard_map/ppermute | solution.py:21
  179.3 6.2 %collective-permute-start.7 = (f32[4,8,2,128]{3,2,1,0:T(2,128)S(1)}, f32[4,8,2,128]{3,2,1,0:T(2,128)S(1)}, u32[]{:S(2)}, u32[]{:S(2)}) collective-permute-start(f32[4,8,2,128]{3,2,1,0:T(2,128)S(1)} %get-tuple-element.40), channel_id=1, source_target_pairs={{1,0},{2,1},{3,2},{0,3},{5,4},{6,5},{7,6},{4,7},{9,8},{10,9},{11,1... | collective-permute-start | bytes 98312 | tf_op jit(solution)/shard_map/ppermute | solution.py:22
  203.2 1.9 copy-start.11
  230.9 64.0 %reduce-scatter.20.cloned.1.call-start = ((), (), s32[]{:S(2)}) async-start(), calls=%async_computation.9 | async-start | bytes 327680
  277.1 62.8 %reduce-scatter.22.cloned.1.call-start = ((), (), s32[]{:S(2)}) async-start(), calls=%async_computation.10 | async-start | bytes 327680
  322.1 139.3 %reduce-scatter.24.cloned.1.call-start = ((), (), s32[]{:S(2)}) async-start(), calls=%async_computation.11 | async-start | bytes 327680
  340.8 87.5 %copy-start.10 = (f32[3,128]{1,0:T(4,128)}, f32[3,128]{1,0:T(4,128)S(1)}, u32[]{:S(2)}) copy-start(f32[3,128]{1,0:T(4,128)S(1)} %multiply_add_fusion.5) | copy-start | bytes 4612
  430.8 66.4 %all-gather.5.cloned.1.call-start = ((), (), s32[]{:S(2)}) async-start(), calls=%async_computation.6 | async-start | bytes 2162688 | tf_op jit(solution)/shard_map/all_gather | solution.py:141
  452.7 46.9 %copy-start.1 = (s32[4096,4]{0,1:T(4,128)S(1)}, s32[4096,4]{0,1:T(4,128)}, u32[]{:S(2)}) copy-start(s32[4096,4]{0,1:T(4,128)} %param.13) | copy-start | bytes 196612
Sparse Core Ops, SparseCore 0:
  52.4 18.9 reduce-scatter.15
  231.0 19.0 reduce-scatter.17
  277.2 17.5 reduce-scatter.19
  322.3 17.6 reduce-scatter.21
  430.9 18.9 reduce-scatter.23
Sparse Core Ops, SparseCore 1:
  128.5 53.1 all-gather.2
  441.7 55.4 all-gather.4
